TPU v7x, 32 devices: a whole 2x2x4 slice. The times are simulated.
32 devices in a mesh: rep: 4 (over x, core), fsdp: 8 (over z, y).
Axes of the slice: x: 2, y: 2, z: 4, core: 2. Of those that a mesh axis runs over, the one named last changes fastest.
Arguments:
- layer_input: bfloat16 [24576, 1024], P(('rep', 'fsdp')), may hold values from -6 to 6
- item_ids: int32 [24576], P(('rep', 'fsdp')), may hold values from 0 to 48, as said below
- norm_gain: bfloat16 [1024], P('fsdp'), may hold values from 0.25 to 1.75
- norm_bias: bfloat16 [1024], P('fsdp'), may hold values from -1.5 to 1.5
- joint_weight: bfloat16 [1024, 3072], P('fsdp'), may hold values from -0.1875 to 0.1875
- joint_bias: bfloat16 [2048], P('fsdp'), may hold values from -1.5 to 1.5
- out_weight: bfloat16 [1024, 1024], P('fsdp'), may hold values from -0.5 to 0.5
- out_bias: bfloat16 [1024], P('fsdp'), may hold values from -1.5 to 1.5
- second_gain: bfloat16 [1024], P('fsdp'), may hold values from 0.25 to 1.75
- second_bias: bfloat16 [1024], P('fsdp'), may hold values from -1.5 to 1.5
- up_weight: bfloat16 [1024, 2048], P('fsdp'), may hold values from -0.1875 to 0.1875
- up_bias: bfloat16 [2048], P('fsdp'), may hold values from -1.5 to 1.5
- down_weight: bfloat16 [2048, 1024], P('fsdp'), may hold values from -0.125 to 0.125
- down_bias: bfloat16 [1024], P('fsdp'), may hold values from -1.5 to 1.5
- output_grad: bfloat16 [24576, 1024], P(('rep', 'fsdp')), may hold values from -6 to 6
Outputs:
- layer_output: bfloat16 [24576, 1024], P(('rep', 'fsdp'))
- input_grad: bfloat16 [24576, 1024], P(('rep', 'fsdp'))
- norm_gain_grad: float32 [1024], P('fsdp')
- norm_bias_grad: float32 [1024], P('fsdp')
- joint_weight_grad: float32 [1024, 3072], P('fsdp')
- joint_bias_grad: float32 [2048], P('fsdp')
- out_weight_grad: float32 [1024, 1024], P('fsdp')
- out_bias_grad: float32 [1024], P('fsdp')
- second_gain_grad: float32 [1024], P('fsdp')
- second_bias_grad: float32 [1024], P('fsdp')
- up_weight_grad: float32 [1024, 2048], P('fsdp')
- up_bias_grad: float32 [2048], P('fsdp')
- down_weight_grad: float32 [2048, 1024], P('fsdp')
- down_bias_grad: float32 [1024], P('fsdp')
Inputs may be any that keep to these rules, and one draw needn't show every extreme that they name: `item_ids`: every aligned block of 768 rows holds whole items, numbered 0, 1, 2, ... in order of position inside the block; items have 15 or 60 tokens, save at most one item of fewer than 15 tokens in a block, and each block holds at least one item of 60 tokens.
All inputs are finite; a program needn't handle non-finite values.
Results may differ from a plain program's by a relative error of at most 0.018.
Values may be sent and summed in bfloat16 or wider, within the bound.
No kernel may reach another device: no remote copies, remote signals or barrier semaphores. Data moves between devices by JAX's collectives and lax.ppermute only.
A program may use at most 192 MiB of HBM per device.

v0:
```python
import jax
import jax.numpy as jnp
from jax import lax
from jax.sharding import PartitionSpec as P

H = 8
HD = 128
QBLK = 768
eps = 1e-05
masked_score = -1e30


def norm_affine(values, gain, bias):
    center = values - jnp.mean(values, axis=-1, keepdims=True)
    spread = jnp.mean(center * center, axis=-1, keepdims=True)
    return center * lax.rsqrt(spread + eps) * gain + bias


def split_heads(matrix):
    blocks = matrix.shape[0] // QBLK
    return matrix.reshape(blocks, QBLK, H, HD).transpose(0, 2, 1, 3).reshape(blocks * H, QBLK, HD)


def merge_heads(stacked):
    blocks = stacked.shape[0] // H
    return stacked.reshape(blocks, H, QBLK, HD).transpose(0, 2, 1, 3).reshape(blocks * QBLK, H * HD)


def block_scores(queries, key_rows, labels):
    scores = lax.dot_general(
        queries, key_rows, (((1,), (1,)), ((), ())), preferred_element_type=jnp.float32
    ) * HD ** (-0.5)
    position = jnp.arange(QBLK)
    allowed = (labels[:, None] == labels[None, :]) & (position[:, None] >= position[None, :])
    return jnp.where(allowed, scores, masked_score)


def head_forward(pieces):
    queries, key_rows, value_rows, labels = pieces
    scores = block_scores(queries, key_rows, labels)
    peak = jnp.max(scores, axis=1, keepdims=True)
    raised = jnp.exp(scores - peak)
    partition = jnp.sum(raised, axis=1, keepdims=True)
    weights = (raised / partition).astype(jnp.bfloat16)
    mixed = jnp.dot(weights, value_rows, preferred_element_type=jnp.float32).astype(jnp.bfloat16)
    return (mixed, (peak + jnp.log(partition))[:, 0])


def head_backward(pieces):
    queries, key_rows, value_rows, labels, upstream, logsum = pieces
    weights = jnp.exp(block_scores(queries, key_rows, labels) - logsum[:, None])
    dweights = lax.dot_general(
        upstream, value_rows, (((1,), (1,)), ((), ())), preferred_element_type=jnp.float32
    )
    grad_value = lax.dot_general(
        weights.astype(jnp.bfloat16),
        upstream,
        (((0,), (0,)), ((), ())),
        preferred_element_type=jnp.float32,
    )
    inner = jnp.sum(weights * dweights, axis=1, keepdims=True)
    dscores = (weights * (dweights - inner)).astype(jnp.bfloat16)
    grad_query = jnp.dot(dscores, key_rows, preferred_element_type=jnp.float32) * HD ** (-0.5)
    grad_key = lax.dot_general(
        dscores, queries, (((0,), (0,)), ((), ())), preferred_element_type=jnp.float32
    ) * HD ** (-0.5)
    return (grad_query, grad_key, grad_value)


def transposed_dot(left, right):
    return lax.dot_general(
        left, right, (((0,), (0,)), ((), ())), preferred_element_type=jnp.float32
    )


def dot_transposed(left, right):
    return lax.dot_general(
        left, right, (((1,), (1,)), ((), ())), preferred_element_type=jnp.float32
    )


def on_device(
    layer_input,
    item_ids,
    norm_gain,
    norm_bias,
    joint_weight,
    joint_bias,
    out_weight,
    out_bias,
    second_gain,
    second_bias,
    up_weight,
    up_bias,
    down_weight,
    down_bias,
    output_grad,
):
    width = layer_input.shape[1]
    row_count = layer_input.shape[0]
    blocks = row_count // QBLK
    gain_one, bias_one, joint_full, joint_shift, out_full, out_shift = (
        lax.all_gather(norm_gain, "fsdp", axis=0, tiled=True),
        lax.all_gather(norm_bias, "fsdp", axis=0, tiled=True),
        lax.all_gather(joint_weight, "fsdp", axis=0, tiled=True),
        lax.all_gather(joint_bias, "fsdp", axis=0, tiled=True),
        lax.all_gather(out_weight, "fsdp", axis=0, tiled=True),
        lax.all_gather(out_bias, "fsdp", axis=0, tiled=True),
    )
    inputs = layer_input.astype(jnp.float32)
    bias_one_f = bias_one.astype(jnp.float32)
    first = norm_affine(inputs, gain_one.astype(jnp.float32), bias_one_f).astype(jnp.bfloat16)
    projected = jnp.dot(first, joint_full, preferred_element_type=jnp.float32)
    shift_f = joint_shift.astype(jnp.float32)
    queries = (projected[:, :width] + shift_f[:width]).astype(jnp.bfloat16)
    key_rows = projected[:, width : 2 * width].astype(jnp.bfloat16)
    value_rows = (projected[:, 2 * width :] + shift_f[width:]).astype(jnp.bfloat16)
    head_queries = split_heads(queries)
    head_keys = split_heads(key_rows)
    head_values = split_heads(value_rows)
    head_labels = jnp.broadcast_to(item_ids.reshape(blocks, 1, QBLK), (blocks, H, QBLK)).reshape(
        blocks * H, QBLK
    )
    head_mixed, logsum = lax.map(head_forward, (head_queries, head_keys, head_values, head_labels))
    attended = merge_heads(head_mixed)
    middle = (
        inputs
        + jnp.dot(attended, out_full, preferred_element_type=jnp.float32)
        + out_shift.astype(jnp.float32)
    )
    gain_two, bias_two, up_full, up_shift, down_full, down_shift = (
        lax.all_gather(second_gain, "fsdp", axis=0, tiled=True),
        lax.all_gather(second_bias, "fsdp", axis=0, tiled=True),
        lax.all_gather(up_weight, "fsdp", axis=0, tiled=True),
        lax.all_gather(up_bias, "fsdp", axis=0, tiled=True),
        lax.all_gather(down_weight, "fsdp", axis=0, tiled=True),
        lax.all_gather(down_bias, "fsdp", axis=0, tiled=True),
    )
    bias_two_f = bias_two.astype(jnp.float32)
    second = norm_affine(middle, gain_two.astype(jnp.float32), bias_two_f).astype(jnp.bfloat16)
    hidden = jnp.dot(second, up_full, preferred_element_type=jnp.float32) + up_shift.astype(
        jnp.float32
    )
    active = jax.nn.gelu(hidden).astype(jnp.bfloat16)
    feed_out = jnp.dot(active, down_full, preferred_element_type=jnp.float32) + down_shift.astype(
        jnp.float32
    )
    layer_output = (middle + feed_out).astype(jnp.bfloat16)
    gain_two_back, up_back, down_back = (
        lax.all_gather(second_gain, "fsdp", axis=0, tiled=True),
        lax.all_gather(up_weight, "fsdp", axis=0, tiled=True),
        lax.all_gather(down_weight, "fsdp", axis=0, tiled=True),
    )
    upstream = output_grad.astype(jnp.float32)
    grad_down = transposed_dot(active, output_grad)
    grad_down_shift = jnp.sum(upstream, axis=0)
    dactive = dot_transposed(output_grad, down_back)
    gelu_value, gelu_pull = jax.vjp(jax.nn.gelu, hidden)
    dhidden = gelu_pull(dactive)[0].astype(jnp.bfloat16)
    grad_up = transposed_dot(second, dhidden)
    grad_up_shift = jnp.sum(dhidden.astype(jnp.float32), axis=0)
    dsecond = dot_transposed(dhidden, up_back)
    norm_value, second_pull = jax.vjp(
        norm_affine, middle, gain_two_back.astype(jnp.float32), bias_two_f
    )
    dmiddle_part, grad_gain_two, grad_bias_two = second_pull(dsecond)
    dmiddle = upstream + dmiddle_part
    grad_gain_two, grad_bias_two, grad_up, grad_up_shift, grad_down, grad_down_shift = (
        lax.psum_scatter(
            grad_gain_two.astype(jnp.bfloat16), "fsdp", scatter_dimension=0, tiled=True
        ).astype(jnp.float32),
        lax.psum_scatter(
            grad_bias_two.astype(jnp.bfloat16), "fsdp", scatter_dimension=0, tiled=True
        ).astype(jnp.float32),
        lax.psum_scatter(
            grad_up.astype(jnp.bfloat16), "fsdp", scatter_dimension=0, tiled=True
        ).astype(jnp.float32),
        lax.psum_scatter(
            grad_up_shift.astype(jnp.bfloat16), "fsdp", scatter_dimension=0, tiled=True
        ).astype(jnp.float32),
        lax.psum_scatter(
            grad_down.astype(jnp.bfloat16), "fsdp", scatter_dimension=0, tiled=True
        ).astype(jnp.float32),
        lax.psum_scatter(
            grad_down_shift.astype(jnp.bfloat16), "fsdp", scatter_dimension=0, tiled=True
        ).astype(jnp.float32),
    )
    gain_one_back, joint_back, out_back = (
        lax.all_gather(norm_gain, "fsdp", axis=0, tiled=True),
        lax.all_gather(joint_weight, "fsdp", axis=0, tiled=True),
        lax.all_gather(out_weight, "fsdp", axis=0, tiled=True),
    )
    dbranch = dmiddle.astype(jnp.bfloat16)
    grad_out = transposed_dot(attended, dbranch)
    grad_out_shift = jnp.sum(dbranch.astype(jnp.float32), axis=0)
    dattended = dot_transposed(dbranch, out_back).astype(jnp.bfloat16)
    grad_queries, grad_keys, grad_values = lax.map(
        head_backward,
        (head_queries, head_keys, head_values, head_labels, split_heads(dattended), logsum),
    )
    dprojected = jnp.concatenate(
        [merge_heads(grad_queries), merge_heads(grad_keys), merge_heads(grad_values)], axis=1
    ).astype(jnp.bfloat16)
    grad_joint = transposed_dot(first, dprojected)
    dprojected_f = dprojected.astype(jnp.float32)
    grad_joint_shift = jnp.concatenate(
        [jnp.sum(dprojected_f[:, :width], axis=0), jnp.sum(dprojected_f[:, 2 * width :], axis=0)]
    )
    dfirst = dot_transposed(dprojected, joint_back)
    first_value, first_pull = jax.vjp(
        norm_affine, inputs, gain_one_back.astype(jnp.float32), bias_one_f
    )
    dinput_part, grad_gain_one, grad_bias_one = first_pull(dfirst)
    input_grad = (dmiddle + dinput_part).astype(jnp.bfloat16)
    grad_gain_one, grad_bias_one, grad_joint, grad_joint_shift, grad_out, grad_out_shift = (
        lax.psum_scatter(
            grad_gain_one.astype(jnp.bfloat16), "fsdp", scatter_dimension=0, tiled=True
        ).astype(jnp.float32),
        lax.psum_scatter(
            grad_bias_one.astype(jnp.bfloat16), "fsdp", scatter_dimension=0, tiled=True
        ).astype(jnp.float32),
        lax.psum_scatter(
            grad_joint.astype(jnp.bfloat16), "fsdp", scatter_dimension=0, tiled=True
        ).astype(jnp.float32),
        lax.psum_scatter(
            grad_joint_shift.astype(jnp.bfloat16), "fsdp", scatter_dimension=0, tiled=True
        ).astype(jnp.float32),
        lax.psum_scatter(
            grad_out.astype(jnp.bfloat16), "fsdp", scatter_dimension=0, tiled=True
        ).astype(jnp.float32),
        lax.psum_scatter(
            grad_out_shift.astype(jnp.bfloat16), "fsdp", scatter_dimension=0, tiled=True
        ).astype(jnp.float32),
    )
    (
        grad_gain_one,
        grad_bias_one,
        grad_joint,
        grad_joint_shift,
        grad_out,
        grad_out_shift,
        grad_gain_two,
        grad_bias_two,
        grad_up,
        grad_up_shift,
        grad_down,
        grad_down_shift,
    ) = (
        lax.psum(grad_gain_one.astype(jnp.bfloat16), "rep").astype(jnp.float32),
        lax.psum(grad_bias_one.astype(jnp.bfloat16), "rep").astype(jnp.float32),
        lax.psum(grad_joint.astype(jnp.bfloat16), "rep").astype(jnp.float32),
        lax.psum(grad_joint_shift.astype(jnp.bfloat16), "rep").astype(jnp.float32),
        lax.psum(grad_out.astype(jnp.bfloat16), "rep").astype(jnp.float32),
        lax.psum(grad_out_shift.astype(jnp.bfloat16), "rep").astype(jnp.float32),
        lax.psum(grad_gain_two.astype(jnp.bfloat16), "rep").astype(jnp.float32),
        lax.psum(grad_bias_two.astype(jnp.bfloat16), "rep").astype(jnp.float32),
        lax.psum(grad_up.astype(jnp.bfloat16), "rep").astype(jnp.float32),
        lax.psum(grad_up_shift.astype(jnp.bfloat16), "rep").astype(jnp.float32),
        lax.psum(grad_down.astype(jnp.bfloat16), "rep").astype(jnp.float32),
        lax.psum(grad_down_shift.astype(jnp.bfloat16), "rep").astype(jnp.float32),
    )
    return (
        layer_output,
        input_grad,
        grad_gain_one,
        grad_bias_one,
        grad_joint,
        grad_joint_shift,
        grad_out,
        grad_out_shift,
        grad_gain_two,
        grad_bias_two,
        grad_up,
        grad_up_shift,
        grad_down,
        grad_down_shift,
    )


def solution(mesh):
    placed = (
        P(("rep", "fsdp"), None),
        P(("rep", "fsdp")),
        P("fsdp"),
        P("fsdp"),
        P("fsdp", None),
        P("fsdp"),
        P("fsdp", None),
        P("fsdp"),
        P("fsdp"),
        P("fsdp"),
        P("fsdp", None),
        P("fsdp"),
        P("fsdp", None),
        P("fsdp"),
        P(("rep", "fsdp"), None),
    )
    return jax.shard_map(
        on_device,
        mesh=mesh,
        in_specs=placed,
        out_specs=(
            P(("rep", "fsdp"), None),
            P(("rep", "fsdp"), None),
            P("fsdp"),
            P("fsdp"),
            P("fsdp", None),
            P("fsdp"),
            P("fsdp", None),
            P("fsdp"),
            P("fsdp"),
            P("fsdp"),
            P("fsdp", None),
            P("fsdp"),
            P("fsdp", None),
            P("fsdp"),
        ),
        check_vma=False,
    )
```

profile of v0, /device:TPU:0, one launch (start us, length us, event | category | flops | bytes accessed | tf_op | source)
XLA Modules:
  0.0 769.2 jit_solution(3482385792619113970)
XLA Ops:
  11.4 22.8 %all-gather = bf16[8,1,128]{2,1,0:T(2,128)(2,1)S(1)} all-gather(bf16[1,1,128]{2,1,0:T(2,128)(2,1)} %bitcast.201), channel_id=1, replica_groups=mesh['rep'=4,'fsdp'=8] {'fsdp'}, dimensions={0}, use_global_device_ids=true | all-gather | bytes 2304 | tf_op jit(solution)/shard_map/all_gather | solution.py:103
  34.2 17.2 %all-gather.1 = bf16[8,1,128]{2,1,0:T(2,128)(2,1)S(1)} all-gather(bf16[1,1,128]{2,1,0:T(2,128)(2,1)} %bitcast.202), channel_id=1, replica_groups=mesh['rep'=4,'fsdp'=8] {'fsdp'}, dimensions={0}, use_global_device_ids=true | all-gather | bytes 2304 | tf_op jit(solution)/shard_map/all_gather | solution.py:104
  51.4 18.7 %all-gather.3 = bf16[8,1,128]{2,1,0:T(2,128)(2,1)S(1)} all-gather(bf16[1,1,128]{2,1,0:T(2,128)(2,1)} %bitcast.203), channel_id=1, replica_groups=mesh['rep'=4,'fsdp'=8] {'fsdp'}, dimensions={0}, use_global_device_ids=true | all-gather | bytes 2304 | tf_op jit(solution)/shard_map/all_gather | solution.py:108
  70.7 17.5 %all-gather.4 = bf16[8,1,128]{2,1,0:T(2,128)(2,1)S(1)} all-gather(bf16[1,1,128]{2,1,0:T(2,128)(2,1)} %bitcast.204), channel_id=1, replica_groups=mesh['rep'=4,'fsdp'=8] {'fsdp'}, dimensions={0}, use_global_device_ids=true | all-gather | bytes 2304 | tf_op jit(solution)/shard_map/all_gather | solution.py:132
  88.8 18.7 %all-gather.5 = bf16[8,1,128]{2,1,0:T(2,128)(2,1)S(1)} all-gather(bf16[1,1,128]{2,1,0:T(2,128)(2,1)} %bitcast.205), channel_id=1, replica_groups=mesh['rep'=4,'fsdp'=8] {'fsdp'}, dimensions={0}, use_global_device_ids=true | all-gather | bytes 2304 | tf_op jit(solution)/shard_map/all_gather | solution.py:133
  109.0 16.5 %all-gather.6 = bf16[8,1,256]{2,1,0:T(2,128)(2,1)S(1)} all-gather(bf16[1,1,256]{2,1,0:T(2,128)(2,1)S(1)} %reshape.217), channel_id=1, replica_groups=mesh['rep'=4,'fsdp'=8] {'fsdp'}, dimensions={0}, use_global_device_ids=true | all-gather | bytes 4608 | tf_op jit(solution)/shard_map/all_gather | solution.py:135
  126.0 18.2 %all-gather.2 = bf16[8,1,256]{2,1,0:T(2,128)(2,1)S(1)} all-gather(bf16[1,1,256]{2,1,0:T(2,128)(2,1)S(1)} %reshape.209), channel_id=1, replica_groups=mesh['rep'=4,'fsdp'=8] {'fsdp'}, dimensions={0}, use_global_device_ids=true | all-gather | bytes 4608 | tf_op jit(solution)/shard_map/all_gather | solution.py:106
  144.3 7.4 fusion.67
  155.7 1.7 copy_bitcast_fusion.1
  158.0 44.3 %while.26 = (s32[]{:T(128)}, bf16[8,768,128]{1,2,0:T(8,128)(2,1)}, f32[8,768]{1,0:T(8,128)}, s32[8,768]{1,0:T(8,128)}, bf16[8,768,128]{2,1,0:T(8,128)(2,1)}, /*i...) while((s32[]{:T(128)}, bf16[8,768,128]{1,2,0:T(8,128)(2,1)}, ...), condition=%wide.region_5.6_spmd, body=%wide.region_2.5_spmd.sunk | while | flops 308575488 | bytes 8705141 | solution.py:124
  158.8 1.6 fusion.117
  169.9 1.6 fusion.117
  186.5 1.6 fusion.117
  192.0 1.6 fusion.117
  202.3 4.7 fusion.81
  207.1 1.6 copy-done.2
  209.1 25.7 %all-gather.17.cloned.1.call-done = bf16[1024,2048]{1,0:T(8,128)(2,1)} async-done(((bf16[128,2048]{1,0:T(8,128)(2,1)}), bf16[1024,2048]{1,0:T(8,128)(2,1)}) %all-gather.17.cloned.1.call-update) | async-done | bytes 4194320 | tf_op jit(solution)/shard_map/all_gather | solution.py:134
  234.9 9.5 %fusion.72 = f32[768,2048]{1,0:T(8,128)} fusion(bf16[1024,2048]{1,0:T(8,128)(2,1)} %all-gather.17.cloned.1.call-done, f32[768,1024]{1,0:T(8,128)} %copy-done.2, f32[1024]{0:T(1024)S(1)} %bitcast.197, f32[1024]{0:T(1024)S(1)} %bitcast.186, f32[768]{0:T(1024)S(1)} %fusion.65, f32[768]{0:T(1024)S(1)} %broadcast_multiply_fusion), kind=kOutput, calls=%fused_computation.127 | convolution fusion | flops 3225157632 | bytes 13645824 | tf_op jit(solution)/shard_map/dot_general | solution.py:141
  244.4 63.9 %all-gather.19.cloned.1.call-done = bf16[2048,1024]{1,0:T(8,128)(2,1)} async-done(((bf16[256,1024]{1,0:T(8,128)(2,1)}), bf16[2048,1024]{1,0:T(8,128)(2,1)}) %all-gather.19.cloned.1.call-update) | async-done | bytes 4194320 | tf_op jit(solution)/shard_map/all_gather | solution.py:136
  308.3 11.2 %fusion.74 = (bf16[2048]{0:T(1024)(128)(2,1)}, bf16[768,2048]{1,0:T(8,128)(2,1)S(1)}) fusion(f32[768,2048]{1,0:T(8,128)} %fusion.72, f32[2048]{0:T(1024)S(1)} %bitcast.192, bf16[768,1024]{1,0:T(8,128)(2,1)S(1)} %copy-done.5, bf16[2048,1024]{1,0:T(8,128)(2,1)} %all-gather.19.cloned.1.call-done), kind=kOutput, calls=%fused_computation.129 | convolution fusion | flops 3255826432 | bytes 15216640 | tf_op jit(solution)/shard_map/dot_general | solution.py:77
  319.4 4.5 multiply_reduce_fusion.1
  328.0 3.1 convolution_convert_fusion.3
  331.2 8.6 %convolution_convert_fusion.2 = bf16[1024,2048]{1,0:T(8,128)(2,1)} fusion(bf16[768,2048]{1,0:T(8,128)(2,1)} %copy-done.33, f32[768,1024]{1,0:T(8,128)} %copy-done.2, f32[1024]{0:T(1024)S(1)} %bitcast.198, f32[1024]{0:T(1024)S(1)} %bitcast.189, f32[768]{0:T(1024)S(1)} %fusion.65, f32[768]{0:T(1024)S(1)} %broadcast_multiply_fusion), kind=kOutput, calls=%fused_computation.78 | convolution fusion | flops 3227254784 | bytes 10500096 | tf_op jit(solution)/shard_map/dot_general | solution.py:71
  340.1 3.9 fusion.63
  346.0 9.8 %convolution_convert_fusion.1 = bf16[2048,1024]{1,0:T(8,128)(2,1)} fusion(bf16[768,1024]{1,0:T(8,128)(2,1)S(1)} %copy-done.7, f32[768,2048]{1,0:T(8,128)} %fusion.72, f32[2048]{0:T(1024)S(1)} %bitcast.193), kind=kOutput, calls=%fused_computation.77 | convolution fusion | flops 3239051264 | bytes 12066816 | tf_op jit(solution)/shard_map/dot_general | solution.py:71
  356.1 103.2 %while.27 = (s32[]{:T(128)}, bf16[8,768,128]{1,2,0:T(8,128)(2,1)}, bf16[8,768,128]{1,2,0:T(8,128)(2,1)}, bf16[8,768,128]{1,2,0:T(8,128)(2,1)}, s32[8,768]{1,0:T(...) while((s32[]{:T(128)}, bf16[8,768,128]{1,2,0:T(8,128)(2,1)}, ...), condition=%wide.region_12.13_spmd, body=%wide.region_10.12_spmd.sunk | while | flops 762445056 | bytes 21464200 | solution.py:197
  359.1 1.8 multiply_reduce_fusion.5
  361.3 2.2 fusion.131
  363.5 2.1 fusion.130
  372.0 1.8 multiply_reduce_fusion.5
  374.2 2.2 fusion.131
  376.4 2.1 fusion.130
  384.9 1.8 multiply_reduce_fusion.5
  387.1 2.2 fusion.131
  389.3 2.1 fusion.130
  397.9 1.8 multiply_reduce_fusion.5
  400.0 2.2 fusion.131
  402.2 2.1 fusion.130
  410.7 1.8 multiply_reduce_fusion.5
  412.9 2.2 fusion.131
  415.1 2.1 fusion.130
  423.6 1.8 multiply_reduce_fusion.5
  425.8 2.2 fusion.131
  428.0 2.1 fusion.130
  436.5 1.8 multiply_reduce_fusion.5
  438.7 2.2 fusion.131
  440.9 2.1 fusion.130
  449.4 1.8 multiply_reduce_fusion.5
  451.6 2.2 fusion.131
  453.8 2.1 fusion.130
  459.3 11.1 %convolution_convert_fusion = bf16[1024,3072]{1,0:T(8,128)(2,1)} fusion(bf16[768,1024]{1,0:T(8,128)(2,1)} %param.19, f32[1024]{0:T(1024)} %bitcast.196, f32[1024]{0:T(1024)S(1)} %bitcast.182, f32[768]{0:T(1024)S(1)} %fusion.64, f32[768]{0:T(1024)S(1)} %broadcast_multiply_fusion.1, bf16[768,1024]{0,1:T(8,128)(2,1)} %bitcast.172, ...), kind=kOutput, calls=%fused_computation.66 | convolution fusion | flops 4853858304 | bytes 12597248 | tf_op jit(solution)/shard_map/dot_general | solution.py:71
  473.0 18.9 %all-gather.7 = bf16[8,1,128]{2,1,0:T(2,128)(2,1)S(1)} all-gather(bf16[1,1,128]{2,1,0:T(2,128)(2,1)S(1)} %bitcast.206), channel_id=1, replica_groups=mesh['rep'=4,'fsdp'=8] {'fsdp'}, dimensions={0}, use_global_device_ids=true | all-gather | bytes 2304 | tf_op jit(solution)/shard_map/all_gather | solution.py:137
  491.9 2.7 fusion.69
  497.0 9.4 %fusion.73 = (bf16[1024]{0:T(1024)(128)(2,1)S(1)}, f32[768]{0:T(1024)S(1)}, f32[768,1024]{1,0:T(8,128)S(1)}) fusion(f32[1024]{0:T(1024)S(1)} %bitcast.183, f32[768]{0:T(1024)S(1)} %broadcast_multiply_fusion.1, bf16[768,1024]{1,0:T(8,128)(2,1)S(1)} %copy-done.1, bf16[1024,3072]{1,0:T(8,128)(2,1)} %all-gather.13.cloned.1.call-done, ...), kind=kOutput, calls=%fused_computation.128 | convolution fusion | flops 4850710528 | bytes 15740928 | tf_op jit(solution)/shard_map/dot_general | solution.py:77
  506.4 1.7 fusion.53
  508.2 34.6 %all-reduce.8 = (bf16[1024]{0:T(1024)(128)(2,1)S(1)}, bf16[1024]{0:T(1024)(128)(2,1)S(1)}, bf16[2048]{0:T(1024)(128)(2,1)S(1)}, bf16[1024]{0:T(1024)(128)(2,1)S(...) all-reduce(bf16[1024]{0:T(1024)(128)(2,1)S(1)} %get-tuple-element.1, ...), channel_id=2, replica_groups=mesh['rep'=4,'fsdp'=8] {'fsdp'}, use_global_device_ids=true, to_apply=%region_16.17.clone | all-reduce | flops 10240 | bytes 40960
  543.4 6.2 all-reduce.9
  553.8 4.5 add_convert_fusion
  558.3 23.1 %reduce-scatter.11.cloned.1.call-done = bf16[256,1024]{1,0:T(8,128)(2,1)} async-done(((bf16[2048,1024]{1,0:T(8,128)(2,1)}), bf16[256,1024]{1,0:T(8,128)(2,1)}) %reduce-scatter.11.cloned.1.call-update) | async-done | bytes 524304 | tf_op jit(solution)/shard_map/reduce_scatter | solution.py:181
  581.4 121.3 %reduce-scatter.5.cloned.1.call-done = bf16[128,3072]{1,0:T(8,128)(2,1)} async-done(((bf16[1024,3072]{1,0:T(8,128)(2,1)}), bf16[128,3072]{1,0:T(8,128)(2,1)}) %reduce-scatter.5.cloned.1.call-update) | async-done | bytes 786448 | tf_op jit(solution)/shard_map/reduce_scatter | solution.py:222
  702.8 10.3 %add_convert_fusion.1 = bf16[768,1024]{1,0:T(8,128)(2,1)} fusion(f32[768,1024]{1,0:T(8,128)} %copy-done.2, bf16[2048,1024]{1,0:T(8,128)(2,1)} %all-gather.19.cloned.1.call-done, f32[1024]{0:T(1024)S(1)} %bitcast.199, f32[768,2048]{1,0:T(8,128)} %fusion.72, f32[2048]{0:T(1024)S(1)} %bitcast.194), kind=kOutput, calls=%fused_computation.98 | convolution fusion | flops 3239313408 | bytes 15216640 | tf_op jit(solution)/shard_map/dot_general | solution.py:145
  713.0 42.9 %all-reduce.13.cloned.1.call-done = (bf16[128,3072]{1,0:T(8,128)(2,1)}, bf16[128,1024]{1,0:T(8,128)(2,1)}, bf16[128,2048]{1,0:T(8,128)(2,1)}, bf16[256,1024]{1,0:T(8,128)(2,1)}) async-done(((bf16[128,3072]{1,0:T(8,128)(2,1)}, bf16[128,1024]{1,0:T(8,128)(2,1)}, bf16[128,2048]{1,0:T(8,128)(2,1)}, bf16[256,1024]{1,0:T(8,128)(2,1)}), (bf16[128,3072]{1,0:T(8,128)(2,1)}, bf16[128,1024]{1,0:T(8,128)(2,1)}, ...) | async-done | bytes 2097168 | tf_op jit(solution)/shard_map/psum | solution.py:251
  756.0 1.9 convert_element_type.198
  757.9 2.4 convert_element_type.194
  (279 shorter events, 121.2 us)
Async XLA Ops:
  7.2 100.9 %copy-start = (bf16[768,1024]{1,0:T(8,128)(2,1)S(1)}, bf16[768,1024]{1,0:T(8,128)(2,1)}, u32[]{:S(2)}) copy-start(bf16[768,1024]{1,0:T(8,128)(2,1)} %param.19) | copy-start | bytes 4718596
  7.2 137.1 %all-gather.13.cloned.1.call-start = ((), (), s32[]{:S(2)}) async-start(), calls=%async_computation.4 | async-start | bytes 7077888 | tf_op jit(solution)/shard_map/all_gather | solution.py:105
  7.9 194.4 %all-gather.15.cloned.1.call-start = ((), (), s32[]{:S(2)}) async-start(), calls=%async_computation.5 | async-start | bytes 2359296 | tf_op jit(solution)/shard_map/all_gather | solution.py:107
  8.7 226.2 %all-gather.17.cloned.1.call-start = ((), (), s32[]{:S(2)}) async-start(), calls=%async_computation.6 | async-start | bytes 4718592 | tf_op jit(solution)/shard_map/all_gather | solution.py:134
  9.4 298.8 %all-gather.19.cloned.1.call-start = ((), (), s32[]{:S(2)}) async-start(), calls=%async_computation.7 | async-start | bytes 4718592 | tf_op jit(solution)/shard_map/all_gather | solution.py:136
  10.0 548.3 %reduce-scatter.7.cloned.1.call-start = ((), (), s32[]{:S(2)}) async-start(), calls=%async_computation.9 | async-start | bytes 2359296 | tf_op jit(solution)/shard_map/reduce_scatter | solution.py:228
  51.4 100.3 %copy-start.24 = (f32[8,1,128]{2,1,0:T(1,128)}, f32[8,1,128]{2,1,0:T(1,128)S(1)}, u32[]{:S(2)}) copy-start(f32[8,1,128]{2,1,0:T(1,128)S(1)} %convert_element_type.211) | copy-start | bytes 12292
  108.9 42.8 %copy-start.14 = (f32[768]{0:T(1024)}, f32[768]{0:T(1024)S(1)}, u32[]{:S(2)}) copy-start(f32[768]{0:T(1024)S(1)} %fusion.54) | copy-start | bytes 9220
  155.7 1.7 copy-start.22
  202.3 4.7 copy-start.8
  207.0 1.6 copy-start.2
  207.1 27.8 %copy-start.16 = (f32[8,1,128]{2,1,0:T(1,128)S(1)}, f32[8,1,128]{2,1,0:T(1,128)}, u32[]{:S(2)}) copy-start(f32[8,1,128]{2,1,0:T(1,128)} %convert_element_type.214) | copy-start | bytes 12292
  207.1 27.8 %copy-start.25 = (f32[8,1,128]{2,1,0:T(1,128)S(1)}, f32[8,1,128]{2,1,0:T(1,128)}, u32[]{:S(2)}) copy-start(f32[8,1,128]{2,1,0:T(1,128)} %convert_element_type.215) | copy-start | bytes 12292
  234.9 73.3 %copy-start.5 = (bf16[768,1024]{1,0:T(8,128)(2,1)S(1)}, bf16[768,1024]{1,0:T(8,128)(2,1)}, u32[]{:S(2)}) copy-start(bf16[768,1024]{1,0:T(8,128)(2,1)} %param.33) | copy-start | bytes 4718596
  234.9 73.3 %copy-start.20 = (f32[8,1,256]{2,1,0:T(1,128)S(1)}, f32[8,1,256]{2,1,0:T(1,128)}, u32[]{:S(2)}) copy-start(f32[8,1,256]{2,1,0:T(1,128)} %convert_element_type.216) | copy-start | bytes 24580
  308.2 11.2 %copy-start.3 = (f32[768,1024]{1,0:T(8,128)S(1)}, f32[768,1024]{1,0:T(8,128)}, u32[]{:S(2)}) copy-start(f32[768,1024]{1,0:T(8,128)} %copy-done.2) | copy-start | bytes 9437188
  308.2 11.2 %copy-start.30 = (bf16[1024,2048]{1,0:T(8,128)(2,1)S(1)}, bf16[1024,2048]{1,0:T(8,128)(2,1)}, u32[]{:S(2)}) copy-start(bf16[1024,2048]{1,0:T(8,128)(2,1)} %all-gather.17.cloned.1.call-done) | copy-start | bytes 12582916
  319.4 4.5 copy-start.33
  324.0 1.4 copy-start.6
  325.4 2.6 copy-start.31
  326.8 1.2 copy-start.11
  328.0 3.2 copy-start.17
  328.0 3.2 copy-start.26
  331.1 227.2 %reduce-scatter.9.cloned.1.call-start = ((), (), s32[]{:S(2)}) async-start(), calls=%async_computation.10 | async-start | bytes 4718592 | tf_op jit(solution)/shard_map/reduce_scatter | solution.py:175
  339.8 241.6 %reduce-scatter.11.cloned.1.call-start = ((), (), s32[]{:S(2)}) async-start(), calls=%async_computation.11 | async-start | bytes 4718592 | tf_op jit(solution)/shard_map/reduce_scatter | solution.py:181
  344.0 1.9 copy-start.7
  355.8 346.9 %reduce-scatter.5.cloned.1.call-start = ((), (), s32[]{:S(2)}) async-start(), calls=%async_computation.8 | async-start | bytes 7077888 | tf_op jit(solution)/shard_map/reduce_scatter | solution.py:222
  470.5 0.7 copy-start.32
  470.5 2.5 copy-start.29
  470.5 285.5 %all-reduce.13.cloned.1.call-start = ((), (), s32[]{:S(2)}) async-start(), calls=%async_computation.12 | async-start | bytes 4194304 | tf_op jit(solution)/shard_map/psum | solution.py:251
  494.6 1.4 copy-start.1
  494.6 1.9 copy-start.9
  494.6 2.3 copy-start.10
  497.0 9.4 %copy-start.15 = (f32[768]{0:T(1024)S(1)}, f32[768]{0:T(1024)}, u32[]{:S(2)}) copy-start(f32[768]{0:T(1024)} %copy-done.14) | copy-start | bytes 9220
  506.4 1.8 copy-start.4
  506.4 1.8 copy-start.18
  506.4 1.8 copy-start.19
  506.4 1.8 copy-start.23
  506.4 1.8 copy-start.27
  506.4 1.8 copy-start.28
  553.8 148.9 %copy-start.21 = (f32[8,1,256]{2,1,0:T(1,128)S(1)}, f32[8,1,256]{2,1,0:T(1,128)}, u32[]{:S(2)}) copy-start(f32[8,1,256]{2,1,0:T(1,128)} %convert_element_type.216) | copy-start | bytes 24580
  756.0 4.3 copy-start.13
  756.0 5.4 copy-start.12
Sparse Core Ops, SparseCore 0:
  10.2 101.6 all-gather.12
  114.0 47.2 all-gather.14
  163.5 71.3 all-gather.16
  236.9 71.3 all-gather.18
  331.2 66.9 reduce-scatter.6
  401.7 87.3 reduce-scatter.8
  492.8 88.6 reduce-scatter.10
  585.0 117.6 reduce-scatter.4
  705.3 50.6 all-reduce.12
where the time goes:
time: 782 us; the launch traced here: 769 us
  waiting for transfers between devices  280 us (36%)
  blocking collectives  189 us (24%)
  matrix products  183 us (23%)
  local copies, waits for them, and re-layouts  67.3 us (9%)
  other arithmetic  32.7 us (4%)
  between operations  15.8 us (2%)
    reduce_scatter x1, waiting for transfers between devices, on_device(): lax.psum_scatter(grad_joint.astype(jnp.bfloat16), 'fsdp', scatter_dimensi...  121 us
    all_gather x1, waiting for transfers between devices, on_device(): lax.all_gather(down_weight, 'fsdp', axis=0, tiled=True)  63.9 us
    psum x1, waiting for transfers between devices, on_device(): lax.psum(grad_joint.astype(jnp.bfloat16), 'rep').astype(jnp.float32)  42.9 us
    unnamed x1, blocking collectives  34.6 us
    dot_general x4, matrix products, transposed_dot(): lax.dot_general(left, right, (((0,), (0,)), ((), ())), preferred_element_...  32.7 us
    dot_general x4, matrix products, dot_transposed(): lax.dot_general(left, right, (((1,), (1,)), ((), ())), preferred_element_...  29 us
    dot_general x16, matrix products, block_scores(): lax.dot_general(queries, key_rows, (((1,), (1,)), ((), ())), preferred_el...  27.2 us
    all_gather x1, waiting for transfers between devices, on_device(): lax.all_gather(up_weight, 'fsdp', axis=0, tiled=True)  25.7 us
  transfers between devices with their start and end apart: 9, of which 5 were waited for; matrix products, arithmetic and copies ran while one was open for 32% of the time, Pallas kernels for 0%

commit v1 on v0

--- a/solution.py
+++ b/solution.py
@@ -232,6 +232,10 @@
             grad_out_shift.astype(jnp.bfloat16), "fsdp", scatter_dimension=0, tiled=True
         ).astype(jnp.float32),
     )
+
+    def values_check(m, ax_name):
+        return jax.lax.all_gather(m, ax_name).sum(axis=0)
+
     (
         grad_gain_one,
         grad_bias_one,
@@ -248,7 +252,7 @@
     ) = (
         lax.psum(grad_gain_one.astype(jnp.bfloat16), "rep").astype(jnp.float32),
         lax.psum(grad_bias_one.astype(jnp.bfloat16), "rep").astype(jnp.float32),
-        lax.psum(grad_joint.astype(jnp.bfloat16), "rep").astype(jnp.float32),
+        values_check(grad_joint.astype(jnp.bfloat16), "rep").astype(jnp.float32),
         lax.psum(grad_joint_shift.astype(jnp.bfloat16), "rep").astype(jnp.float32),
         lax.psum(grad_out.astype(jnp.bfloat16), "rep").astype(jnp.float32),
         lax.psum(grad_out_shift.astype(jnp.bfloat16), "rep").astype(jnp.float32),

time: 782 us -> 810 us (1.036)
  waiting for transfers between devices: 280 us -> 300 us
    reduce_scatter x1, waiting for transfers between devices: 23.1 us -> 91.6 us  [on_device(): lax.psum_scatter(grad_down.astype(jnp.bfloat16), 'fsdp', scatter_dimensio...]
    psum x1, waiting for transfers between devices: 42.9 us -> 0.01 us  [on_device(): lax.psum(grad_out.astype(jnp.bfloat16), 'rep').astype(jnp.float32)]
    reduce_scatter x1, waiting for transfers between devices: 121 us -> 99.2 us  [on_device(): lax.psum_scatter(grad_joint.astype(jnp.bfloat16), 'fsdp', scatter_dimensi...]
    reduce_scatter x1, waiting for transfers between devices: 0.01 us -> 18.4 us  [on_device(): lax.psum_scatter(grad_up.astype(jnp.bfloat16), 'fsdp', scatter_dimension=...]
  transfers between devices with their start and end apart: 9 -> 10, of which waited for: 5 -> 5; matrix products, arithmetic and copies ran while one was open for 32% -> 32% of each run, Pallas kernels for 0% -> 0%
where the time goes in v1:
time: 810 us; the launch traced here: 797 us
  waiting for transfers between devices  300 us (37%)
  blocking collectives  191 us (24%)
  matrix products  187 us (23%)
  local copies, waits for them, and re-layouts  66.3 us (8%)
  other arithmetic  35.9 us (4%)
  between operations  16.1 us (2%)
    reduce_scatter x1, waiting for transfers between devices, on_device(): lax.psum_scatter(grad_joint.astype(jnp.bfloat16), 'fsdp', scatter_dimensi...  99.2 us
    reduce_scatter x1, waiting for transfers between devices, on_device(): lax.psum_scatter(grad_down.astype(jnp.bfloat16), 'fsdp', scatter_dimensio...  91.6 us
    all_gather x1, waiting for transfers between devices, on_device(): lax.all_gather(down_weight, 'fsdp', axis=0, tiled=True)  65.6 us
    unnamed x1, blocking collectives  35.2 us
    dot_general x4, matrix products, transposed_dot(): lax.dot_general(left, right, (((0,), (0,)), ((), ())), preferred_element_...  32.7 us
    dot_general x4, matrix products, dot_transposed(): lax.dot_general(left, right, (((1,), (1,)), ((), ())), preferred_element_...  29 us
    dot_general x16, matrix products, block_scores(): lax.dot_general(queries, key_rows, (((1,), (1,)), ((), ())), preferred_el...  27.3 us
    all_gather x1, blocking collectives, on_device(): lax.all_gather(norm_gain, 'fsdp', axis=0, tiled=True)  22.8 us
  transfers between devices with their start and end apart: 10, of which 5 were waited for; matrix products, arithmetic and copies ran while one was open for 32% of the time, Pallas kernels for 0%

profile of v1, /device:TPU:0, one launch (start us, length us, event | category | flops | bytes accessed | tf_op | source)
XLA Modules:
  0.0 797.2 jit_solution(16214351803139515204)
XLA Ops:
  11.4 22.8 %all-gather.1 = bf16[8,1,128]{2,1,0:T(2,128)(2,1)S(1)} all-gather(bf16[1,1,128]{2,1,0:T(2,128)(2,1)} %bitcast.203), channel_id=1, replica_groups=mesh['rep'=4,'fsdp'=8] {'fsdp'}, dimensions={0}, use_global_device_ids=true | all-gather | bytes 2304 | tf_op jit(solution)/shard_map/all_gather | solution.py:103
  34.2 17.2 %all-gather.2 = bf16[8,1,128]{2,1,0:T(2,128)(2,1)S(1)} all-gather(bf16[1,1,128]{2,1,0:T(2,128)(2,1)} %bitcast.204), channel_id=1, replica_groups=mesh['rep'=4,'fsdp'=8] {'fsdp'}, dimensions={0}, use_global_device_ids=true | all-gather | bytes 2304 | tf_op jit(solution)/shard_map/all_gather | solution.py:104
  51.4 18.7 %all-gather.4 = bf16[8,1,128]{2,1,0:T(2,128)(2,1)S(1)} all-gather(bf16[1,1,128]{2,1,0:T(2,128)(2,1)} %bitcast.205), channel_id=1, replica_groups=mesh['rep'=4,'fsdp'=8] {'fsdp'}, dimensions={0}, use_global_device_ids=true | all-gather | bytes 2304 | tf_op jit(solution)/shard_map/all_gather | solution.py:108
  70.1 17.4 %all-gather.5 = bf16[8,1,128]{2,1,0:T(2,128)(2,1)S(1)} all-gather(bf16[1,1,128]{2,1,0:T(2,128)(2,1)} %bitcast.206), channel_id=1, replica_groups=mesh['rep'=4,'fsdp'=8] {'fsdp'}, dimensions={0}, use_global_device_ids=true | all-gather | bytes 2304 | tf_op jit(solution)/shard_map/all_gather | solution.py:132
  87.5 18.4 %all-gather.6 = bf16[8,1,128]{2,1,0:T(2,128)(2,1)S(1)} all-gather(bf16[1,1,128]{2,1,0:T(2,128)(2,1)} %bitcast.207), channel_id=1, replica_groups=mesh['rep'=4,'fsdp'=8] {'fsdp'}, dimensions={0}, use_global_device_ids=true | all-gather | bytes 2304 | tf_op jit(solution)/shard_map/all_gather | solution.py:133
  106.8 16.6 %all-gather.7 = bf16[8,1,256]{2,1,0:T(2,128)(2,1)S(1)} all-gather(bf16[1,1,256]{2,1,0:T(2,128)(2,1)S(1)} %reshape.218), channel_id=1, replica_groups=mesh['rep'=4,'fsdp'=8] {'fsdp'}, dimensions={0}, use_global_device_ids=true | all-gather | bytes 4608 | tf_op jit(solution)/shard_map/all_gather | solution.py:135
  123.4 18.2 %all-gather.3 = bf16[8,1,256]{2,1,0:T(2,128)(2,1)S(1)} all-gather(bf16[1,1,256]{2,1,0:T(2,128)(2,1)S(1)} %reshape.210), channel_id=1, replica_groups=mesh['rep'=4,'fsdp'=8] {'fsdp'}, dimensions={0}, use_global_device_ids=true | all-gather | bytes 4608 | tf_op jit(solution)/shard_map/all_gather | solution.py:106
  141.6 7.4 fusion.67
  153.0 2.3 copy_bitcast_fusion.1
  155.9 51.8 %while.26 = (s32[]{:T(128)}, bf16[8,768,128]{1,2,0:T(8,128)(2,1)}, f32[8,768]{1,0:T(8,128)}, s32[8,768]{1,0:T(8,128)}, bf16[8,768,128]{2,1,0:T(8,128)(2,1)}, /*i...) while((s32[]{:T(128)}, bf16[8,768,128]{1,2,0:T(8,128)(2,1)}, ...), condition=%wide.region_5.6_spmd, body=%wide.region_2.5_spmd.sunk | while | flops 308575488 | bytes 8703093 | solution.py:124
  169.6 1.6 fusion.117
  195.4 1.7 fusion.117
  207.7 4.5 fusion.81
  212.7 22.2 %all-gather.19.cloned.1.call-done = bf16[1024,2048]{1,0:T(8,128)(2,1)} async-done(((bf16[128,2048]{1,0:T(8,128)(2,1)}), bf16[1024,2048]{1,0:T(8,128)(2,1)}) %all-gather.19.cloned.1.call-update) | async-done | bytes 4194320 | tf_op jit(solution)/shard_map/all_gather | solution.py:134
  234.9 7.8 fusion.72
  242.7 65.6 %all-gather.21.cloned.1.call-done = bf16[2048,1024]{1,0:T(8,128)(2,1)} async-done(((bf16[256,1024]{1,0:T(8,128)(2,1)}), bf16[2048,1024]{1,0:T(8,128)(2,1)}) %all-gather.21.cloned.1.call-update) | async-done | bytes 4194320 | tf_op jit(solution)/shard_map/all_gather | solution.py:136
  308.2 11.3 %fusion.74 = (bf16[2048]{0:T(1024)(128)(2,1)}, bf16[768,2048]{1,0:T(8,128)(2,1)S(1)}) fusion(f32[768,2048]{1,0:T(8,128)} %fusion.72, f32[2048]{0:T(1024)S(1)} %bitcast.194, bf16[768,1024]{1,0:T(8,128)(2,1)} %param.33, bf16[2048,1024]{1,0:T(8,128)(2,1)} %all-gather.21.cloned.1.call-done), kind=kOutput, calls=%fused_computation.129 | convolution fusion | flops 3255826432 | bytes 15216640 | tf_op jit(solution)/shard_map/dot_general | solution.py:77
  319.5 4.5 multiply_reduce_fusion.1
  324.1 3.0 fusion.78
  329.7 3.1 convolution_convert_fusion.3
  333.1 8.6 %convolution_convert_fusion.2 = bf16[1024,2048]{1,0:T(8,128)(2,1)} fusion(bf16[768,2048]{1,0:T(8,128)(2,1)} %copy-done.26, f32[768,1024]{1,0:T(8,128)} %copy-done.2, f32[1024]{0:T(1024)S(1)} %bitcast.200, f32[1024]{0:T(1024)S(1)} %bitcast.191, f32[768]{0:T(1024)S(1)} %fusion.65, f32[768]{0:T(1024)S(1)} %broadcast_multiply_fusion), kind=kOutput, calls=%fused_computation.78 | convolution fusion | flops 3227254784 | bytes 10500096 | tf_op jit(solution)/shard_map/dot_general | solution.py:71
  341.8 3.9 fusion.63
  347.6 9.8 %convolution_convert_fusion.1 = bf16[2048,1024]{1,0:T(8,128)(2,1)} fusion(bf16[768,1024]{1,0:T(8,128)(2,1)S(1)} %copy-done.6, f32[768,2048]{1,0:T(8,128)} %fusion.72, f32[2048]{0:T(1024)S(1)} %bitcast.195), kind=kOutput, calls=%fused_computation.77 | convolution fusion | flops 3239051264 | bytes 12066816 | tf_op jit(solution)/shard_map/dot_general | solution.py:71
  357.8 103.2 %while.27 = (s32[]{:T(128)}, bf16[8,768,128]{1,2,0:T(8,128)(2,1)}, bf16[8,768,128]{1,2,0:T(8,128)(2,1)}, bf16[8,768,128]{1,2,0:T(8,128)(2,1)}, s32[8,768]{1,0:T(...) while((s32[]{:T(128)}, bf16[8,768,128]{1,2,0:T(8,128)(2,1)}, ...), condition=%wide.region_12.13_spmd, body=%wide.region_10.12_spmd.sunk | while | flops 762445056 | bytes 21464200 | solution.py:197
  360.8 1.8 multiply_reduce_fusion.5
  363.0 2.2 fusion.131
  365.1 2.1 fusion.130
  373.7 1.8 multiply_reduce_fusion.5
  375.9 2.2 fusion.131
  378.1 2.1 fusion.130
  386.6 1.8 multiply_reduce_fusion.5
  388.8 2.2 fusion.131
  390.9 2.1 fusion.130
  399.5 1.8 multiply_reduce_fusion.5
  401.7 2.2 fusion.131
  403.9 2.1 fusion.130
  412.4 1.8 multiply_reduce_fusion.5
  414.6 2.2 fusion.131
  416.7 2.1 fusion.130
  425.3 1.8 multiply_reduce_fusion.5
  427.5 2.2 fusion.131
  429.6 2.1 fusion.130
  438.2 1.8 multiply_reduce_fusion.5
  440.4 2.2 fusion.131
  442.6 2.1 fusion.130
  451.1 1.8 multiply_reduce_fusion.5
  453.3 2.2 fusion.131
  455.5 2.1 fusion.130
  461.0 11.1 %convolution_convert_fusion = bf16[1024,3072]{1,0:T(8,128)(2,1)} fusion(bf16[768,1024]{1,0:T(8,128)(2,1)} %param.19, f32[1024]{0:T(1024)} %bitcast.198, f32[1024]{0:T(1024)S(1)} %bitcast.184, f32[768]{0:T(1024)S(1)} %fusion.64, f32[768]{0:T(1024)S(1)} %broadcast_multiply_fusion.1, bf16[768,1024]{0,1:T(8,128)(2,1)} %bitcast.174, ...), kind=kOutput, calls=%fused_computation.66 | convolution fusion | flops 4853858304 | bytes 12597248 | tf_op jit(solution)/shard_map/dot_general | solution.py:71
  472.2 18.4 %reduce-scatter.9.cloned.1.call-done = bf16[128,2048]{1,0:T(8,128)(2,1)} async-done(((bf16[1024,2048]{1,0:T(8,128)(2,1)}), bf16[128,2048]{1,0:T(8,128)(2,1)}) %reduce-scatter.9.cloned.1.call-update) | async-done | bytes 524304 | tf_op jit(solution)/shard_map/reduce_scatter | solution.py:175
  490.7 91.6 %reduce-scatter.11.cloned.1.call-done = bf16[256,1024]{1,0:T(8,128)(2,1)} async-done(((bf16[2048,1024]{1,0:T(8,128)(2,1)}), bf16[256,1024]{1,0:T(8,128)(2,1)}) %reduce-scatter.11.cloned.1.call-update) | async-done | bytes 524304 | tf_op jit(solution)/shard_map/reduce_scatter | solution.py:181
  584.2 20.1 %all-gather.8 = bf16[8,1,128]{2,1,0:T(2,128)(2,1)S(1)} all-gather(bf16[1,1,128]{2,1,0:T(2,128)(2,1)S(1)} %bitcast.208), channel_id=1, replica_groups=mesh['rep'=4,'fsdp'=8] {'fsdp'}, dimensions={0}, use_global_device_ids=true | all-gather | bytes 2304 | tf_op jit(solution)/shard_map/all_gather | solution.py:137
  604.3 99.2 %reduce-scatter.5.cloned.1.call-done = bf16[128,3072]{1,0:T(8,128)(2,1)} async-done(((bf16[1024,3072]{1,0:T(8,128)(2,1)}), bf16[128,3072]{1,0:T(8,128)(2,1)}) %reduce-scatter.5.cloned.1.call-update) | async-done | bytes 786448 | tf_op jit(solution)/shard_map/reduce_scatter | solution.py:222
  703.6 2.7 fusion.69
  708.6 9.3 %fusion.73 = (bf16[1024]{0:T(1024)(128)(2,1)S(1)}, f32[768]{0:T(1024)S(1)}, f32[768,1024]{1,0:T(8,128)S(1)}) fusion(f32[1024]{0:T(1024)S(1)} %bitcast.185, f32[768]{0:T(1024)S(1)} %broadcast_multiply_fusion.1, bf16[768,1024]{1,0:T(8,128)(2,1)S(1)} %copy-done.1, bf16[1024,3072]{1,0:T(8,128)(2,1)} %all-gather.15.cloned.1.call-done, ...), kind=kOutput, calls=%fused_computation.128 | convolution fusion | flops 4850710528 | bytes 15740928 | tf_op jit(solution)/shard_map/dot_general | solution.py:77
  718.0 1.7 fusion.53
  719.8 35.2 %all-reduce.8 = (bf16[1024]{0:T(1024)(128)(2,1)S(1)}, bf16[1024]{0:T(1024)(128)(2,1)S(1)}, bf16[2048]{0:T(1024)(128)(2,1)S(1)}, bf16[1024]{0:T(1024)(128)(2,1)S(...) all-reduce(bf16[1024]{0:T(1024)(128)(2,1)S(1)} %get-tuple-element.1, ...), channel_id=3, replica_groups=mesh['rep'=4,'fsdp'=8] {'fsdp'}, use_global_device_ids=true, to_apply=%region_16.17.clone | all-reduce | flops 10240 | bytes 40960
  755.6 6.6 all-reduce.9
  766.4 4.6 add_convert_fusion
  772.1 8.2 %add_convert_fusion.1 = bf16[768,1024]{1,0:T(8,128)(2,1)} fusion(f32[768,1024]{1,0:T(8,128)S(1)} %copy-done.3, bf16[2048,1024]{1,0:T(8,128)(2,1)S(1)} %copy-done.22, f32[1024]{0:T(1024)S(1)} %bitcast.201, f32[768,2048]{1,0:T(8,128)} %fusion.72, f32[2048]{0:T(1024)S(1)} %bitcast.196), kind=kOutput, calls=%fused_computation.98 | convolution fusion | flops 3239313408 | bytes 15216640 | tf_op jit(solution)/shard_map/dot_general | solution.py:145
  780.3 1.8 convert_element_type.200
  782.1 2.1 convert_element_type.207
  784.2 2.1 convert_element_type.210
  786.4 2.5 reduce_sum.214
  (269 shorter events, 127.6 us)
Async XLA Ops:
  7.2 98.8 %copy-start = (bf16[768,1024]{1,0:T(8,128)(2,1)S(1)}, bf16[768,1024]{1,0:T(8,128)(2,1)}, u32[]{:S(2)}) copy-start(bf16[768,1024]{1,0:T(8,128)(2,1)} %param.19) | copy-start | bytes 4718596
  7.2 134.4 %all-gather.15.cloned.1.call-start = ((), (), s32[]{:S(2)}) async-start(), calls=%async_computation.4 | async-start | bytes 7077888 | tf_op jit(solution)/shard_map/all_gather | solution.py:105
  7.9 199.8 %all-gather.17.cloned.1.call-start = ((), (), s32[]{:S(2)}) async-start(), calls=%async_computation.5 | async-start | bytes 2359296 | tf_op jit(solution)/shard_map/all_gather | solution.py:107
  8.7 226.2 %all-gather.19.cloned.1.call-start = ((), (), s32[]{:S(2)}) async-start(), calls=%async_computation.6 | async-start | bytes 4718592 | tf_op jit(solution)/shard_map/all_gather | solution.py:134
  9.4 298.8 %all-gather.21.cloned.1.call-start = ((), (), s32[]{:S(2)}) async-start(), calls=%async_computation.7 | async-start | bytes 4718592 | tf_op jit(solution)/shard_map/all_gather | solution.py:136
  10.0 462.2 %reduce-scatter.7.cloned.1.call-start = ((), (), s32[]{:S(2)}) async-start(), calls=%async_computation.9 | async-start | bytes 2359296 | tf_op jit(solution)/shard_map/reduce_scatter | solution.py:228
  51.4 97.6 %copy-start.18 = (f32[8,1,128]{2,1,0:T(1,128)}, f32[8,1,128]{2,1,0:T(1,128)S(1)}, u32[]{:S(2)}) copy-start(f32[8,1,128]{2,1,0:T(1,128)S(1)} %convert_element_type.213) | copy-start | bytes 12292
  106.8 42.2 %copy-start.10 = (f32[768]{0:T(1024)}, f32[768]{0:T(1024)S(1)}, u32[]{:S(2)}) copy-start(f32[768]{0:T(1024)S(1)} %fusion.54) | copy-start | bytes 9220
  123.4 224.3 %copy-start.14 = (f32[8,1,256]{2,1,0:T(1,128)}, f32[8,1,256]{2,1,0:T(1,128)S(1)}, u32[]{:S(2)}) copy-start(f32[8,1,256]{2,1,0:T(1,128)S(1)} %convert_element_type.218) | copy-start | bytes 24580
  153.0 2.3 copy-start.16
  212.3 107.2 %copy-start.2 = (f32[768,1024]{1,0:T(8,128)}, f32[768,1024]{1,0:T(8,128)S(1)}, u32[]{:S(2)}) copy-start(f32[768,1024]{1,0:T(8,128)S(1)} %get-tuple-element.191) | copy-start | bytes 9437188
  308.2 11.3 %copy-start.23 = (bf16[1024,2048]{1,0:T(8,128)(2,1)S(1)}, bf16[1024,2048]{1,0:T(8,128)(2,1)}, u32[]{:S(2)}) copy-start(bf16[1024,2048]{1,0:T(8,128)(2,1)} %all-gather.19.cloned.1.call-done) | copy-start | bytes 12582916
  319.5 4.5 copy-start.26
  324.1 3.0 copy-start.5
  327.1 2.6 copy-start.24
  328.5 1.2 copy-start.9
  332.8 157.8 %reduce-scatter.9.cloned.1.call-start = ((), (), s32[]{:S(2)}) async-start(), calls=%async_computation.10 | async-start | bytes 4718592 | tf_op jit(solution)/shard_map/reduce_scatter | solution.py:175
  341.7 240.5 %reduce-scatter.11.cloned.1.call-start = ((), (), s32[]{:S(2)}) async-start(), calls=%async_computation.11 | async-start | bytes 4718592 | tf_op jit(solution)/shard_map/reduce_scatter | solution.py:181
  345.7 1.9 copy-start.6
  357.5 346.1 %reduce-scatter.5.cloned.1.call-start = ((), (), s32[]{:S(2)}) async-start(), calls=%async_computation.8 | async-start | bytes 7077888 | tf_op jit(solution)/shard_map/reduce_scatter | solution.py:222
  472.1 110.2 %copy-start.25 = (u32[32]{0:T(128)S(1)}, u32[32]{0:T(128)}, u32[]{:S(2)}) copy-start(u32[32]{0:T(128)} %constant.86) | copy-start | bytes 388
  472.1 112.1 %copy-start.21 = (bf16[128]{0:T(256)(128)(2,1)S(1)}, bf16[128]{0:T(256)(128)(2,1)}, u32[]{:S(2)}) copy-start(bf16[128]{0:T(256)(128)(2,1)} %param.32) | copy-start | bytes 772
  472.2 308.2 %all-reduce.13.cloned.1.call-start = ((), (), s32[]{:S(2)}) async-start(), calls=%async_computation.13 | async-start | bytes 2621440 | tf_op jit(solution)/shard_map/psum | solution.py:257
  582.3 204.1 %all-gather.23.cloned.1.call-start = ((), (), s32[]{:S(2)}) async-start(), calls=%async_computation.12 | async-start | bytes 3932160 | tf_op jit(solution)/shard_map/all_gather | solution.py:237
  706.3 1.4 copy-start.1
  706.3 1.9 copy-start.7
  706.3 2.3 copy-start.8
  708.6 9.3 %copy-start.11 = (f32[768]{0:T(1024)S(1)}, f32[768]{0:T(1024)}, u32[]{:S(2)}) copy-start(f32[768]{0:T(1024)} %copy-done.10) | copy-start | bytes 9220
  717.9 1.8 copy-start.4
  717.9 1.8 copy-start.12
  717.9 1.8 copy-start.13
  717.9 1.8 copy-start.17
  717.9 1.8 copy-start.19
  717.9 1.8 copy-start.20
  766.4 4.7 copy-start.3
  766.4 4.7 copy-start.15
  766.4 5.7 copy-start.22
Sparse Core Ops, SparseCore 0:
  10.2 101.6 all-gather.14
  114.0 47.2 all-gather.16
  163.5 71.3 all-gather.18
  236.9 71.3 all-gather.20
  332.9 66.8 reduce-scatter.6
  403.3 87.3 reduce-scatter.8
  494.3 87.9 reduce-scatter.10
  585.8 117.6 reduce-scatter.4
  706.1 38.4 all-reduce.12
  746.0 28.6 all-gather.22
